TPU v7x, 128 devices: a whole 4x4x4 slice. The times are simulated.
128 devices in a mesh: band: 4 (over z_lo, core), pos: 32 (over z_hi, y, x).
Axes of the slice: x: 4, y: 4, z: 4 (z_hi: 2, z_lo: 2; z = z_hi * 2 + z_lo), core: 2. Of those that a mesh axis runs over, the one named last changes fastest.
Arguments:
- input_map: bfloat16 [1, 32, 4, 64, 4096], P(None, 'pos', 'band'), may hold values from -6 to 6
- cotangent: bfloat16 [1, 32, 4, 64, 4096], P(None, 'pos', 'band'), may hold values from -6 to 6
- band_width: int32 [32], P('pos'), may hold values from 2 to 3
- dilation: int32 [2], replicated, may hold values from 1 to 16, as said below
- conv_weight: bfloat16 [2, 64, 576], replicated, may hold values from -0.25 to 0.25
- conv_bias: float32 [2, 64], replicated, may hold values from -3 to 3
Outputs:
- output_map: bfloat16 [1, 32, 4, 64, 4096], P(None, 'pos', 'band')
- input_grad: float32 [1, 32, 4, 64, 4096], P(None, 'pos', 'band')
- weight_grad: float32 [2, 64, 576], replicated
- bias_grad: float32 [2, 64], replicated
Inputs may be any that keep to these rules, and one draw needn't show every extreme that they name: Some layer has dilation exactly 16.
All inputs are finite; a program needn't handle non-finite values.
Results may differ from a plain program's by a relative error of at most 0.0075.
Values may be sent and summed in bfloat16 or wider, within the bound.
A program may use at most 128 MiB of HBM per device.

v0:
```python
import functools
import math

import jax
import jax.numpy as jnp
from jax import lax
from jax.experimental import pallas as pl
from jax.experimental.pallas import tpu as pltpu
from jax.sharding import PartitionSpec as P

BLOCK = 64
DMAX = 16
LAYERS = 2
BWD = 8
SLOTS = 2
CH = 64
LANES = 128
HALF = 32
WIDE = BLOCK + 2 * DMAX
F32 = jnp.float32
BF16 = jnp.bfloat16
MESH = pl.DeviceIdType.MESH

STEPS = ((1, -1), (0, -1), (0, 1), (-1, 1), (1, 0), (1, -2), (-1, 2), (-1, 0))
ABOVE, RIGHT, LEFT, BELOW, CORNER_ABOVE, FAR_ABOVE, FAR_BELOW, CORNER_BELOW = range(8)
EDGE_LOW = slice(0, DMAX)
CENTRE = slice(DMAX, DMAX + BLOCK)
EDGE_HIGH = slice(DMAX + BLOCK, WIDE)
SQRT_2_PI = math.sqrt(2.0 / math.pi)
CUBIC = 0.044715


def is_low(shape):
    return lax.broadcasted_iota(jnp.int32, shape, len(shape) - 1) < CH


def swap(value):
    return pltpu.roll(value, CH, value.ndim - 1)


def pick(low_value, high_value):
    return jnp.where(is_low(low_value.shape), low_value, high_value)


def merge(first, second):
    return jnp.concatenate([pick(first, swap(second)), pick(swap(first), second)], axis=0)


def both_gelu(value):
    square = value * value
    inner = SQRT_2_PI * (value + CUBIC * (square * value))
    bend = jnp.tanh(inner)
    cdf = 0.5 * (1.0 + bend)
    slope = cdf + 0.5 * value * (1.0 - bend * bend) * (SQRT_2_PI * (1.0 + 3.0 * CUBIC * square))
    return value * cdf, slope


def net_kernel(
    rows_all,
    offsets_all,
    scale,
    width_ref,
    dilation_ref,
    input_ref,
    cot_ref,
    weight_ref,
    bias_ref,
    out_ref,
    grad_ref,
    sums_ref,
    frame,
    term_ref,
    slots,
    shards,
    whole,
    cols,
    slopes,
    slope_low,
    padded,
    grad,
    above,
    below,
    pair_grad,
    w_fwd,
    w_bwd,
    turn,
    send_a,
    send_b,
    send_l,
    send_r,
    send_c,
    recv_a,
    recv_b,
    recv_l,
    recv_r,
    recv_c,
    send_sem,
    recv_sem,
    sum_send,
    sum_recv,
):
    row = lax.axis_index("pos")
    off = lax.axis_index("band")

    def exists(di, do):
        return (row + di >= 0) & (row + di < rows_all) & (off + do >= 0) & (off + do < offsets_all)

    group = whole.shape[0]
    many = shards.shape[0]
    rows = term_ref.shape[1]
    inner = lax.rem(row, group)
    high = lax.div(row, group)
    mine = high * offsets_all + off

    def in_plane(step):
        other = lax.rem(inner + step, group)
        return other, {"pos": high * group + other, "band": off}

    def across(step):
        other = lax.rem(mine + step, many)
        return other, {
            "pos": lax.div(other, offsets_all) * group + inner,
            "band": lax.rem(other, offsets_all),
        }

    kept = jnp.where(
        (off <= width_ref[0]) & (row + off < rows_all), jnp.float32(1.0), jnp.float32(0.0)
    )

    first, final = slice(0, DMAX), slice(BLOCK - DMAX, BLOCK)
    strips = {
        ABOVE: (send_a, recv_a),
        RIGHT: (send_r, recv_r),
        LEFT: (send_l, recv_l),
        BELOW: (send_b, recv_b),
    }
    corners = {
        CORNER_ABOVE: (send_a, final),
        FAR_ABOVE: (send_a, first),
        FAR_BELOW: (send_b, final),
        CORNER_BELOW: (send_b, first),
    }

    def arrival(index, piece):
        if piece in corners:
            return recv_c.at[index, piece - 4]
        return strips[piece][1].at[index]

    def departure(index, piece):
        if piece in strips:
            return strips[piece][0].at[index]
        if index < LAYERS:
            source, part = corners[piece]
            return source.at[index, :, part, :]
        return send_c.at[index - LAYERS, piece - 4]

    for piece in range(8):
        di, do = STEPS[piece]
        for sign, indices in ((1, (0, 1)), (-1, (2, 3))):

            @pl.when(jnp.logical_not(exists(-sign * di, -sign * do)))
            def _():
                for index in indices:
                    there = arrival(index, piece)
                    there[...] = jnp.zeros(there.shape, BF16)

    barrier = pltpu.get_barrier_semaphore()
    count = jnp.int32(0)
    for di, do in STEPS:
        count = count + exists(di, do).astype(jnp.int32)

        @pl.when(exists(di, do))
        def _():
            pl.semaphore_signal(
                barrier,
                inc=1,
                device_id={"pos": row + di, "band": off + do},
                device_id_type=MESH,
            )

    for step in range(1, group):
        pl.semaphore_signal(barrier, inc=1, device_id=in_plane(step)[1], device_id_type=MESH)
    for step in range(1, many):
        pl.semaphore_signal(barrier, inc=1, device_id=across(step)[1], device_id_type=MESH)
    count = count + (group + many - 2)

    def piece_copy(index, piece):
        di, do = STEPS[piece]
        sign = 1 if index < LAYERS else -1
        return pltpu.make_async_remote_copy(
            src_ref=departure(index, piece),
            dst_ref=arrival(index, piece),
            send_sem=send_sem.at[index, piece],
            recv_sem=recv_sem.at[index, piece],
            device_id={"pos": row + sign * di, "band": off + sign * do},
            device_id_type=MESH,
        )

    def send(index, pieces):
        sign = 1 if index < LAYERS else -1
        for piece in pieces:
            di, do = STEPS[piece]

            @pl.when(exists(sign * di, sign * do))
            def _():
                piece_copy(index, piece).start()

    def wait(index, pieces):
        sign = 1 if index < LAYERS else -1
        for piece in pieces:
            di, do = STEPS[piece]

            @pl.when(exists(-sign * di, -sign * do))
            def _():
                piece_copy(index, piece).wait_recv()

    def finish(index):
        sign = 1 if index < LAYERS else -1
        for piece in range(8):
            di, do = STEPS[piece]

            @pl.when(exists(sign * di, sign * do))
            def _():
                piece_copy(index, piece).wait_send()

    def to_tiles(source, k):
        first = source[:, pl.ds(pl.multiple_of(k * LANES, LANES), LANES)].astype(F32)
        second = source[:, pl.ds(pl.multiple_of((k + 16) * LANES, LANES), LANES)].astype(F32)
        return jnp.concatenate([first, second], axis=0).T

    def rows_to_cols(load, store):
        @pl.loop(0, 8, unroll=8)
        def _(k):
            turn[pl.ds(pl.multiple_of(k * 64, 64), 64), :] = load(k)

        for t in range(HALF):
            store(t, merge(turn[pl.ds(t, 8, stride=64), :], turn[pl.ds(HALF + t, 8, stride=64), :]))

    def cols_to_rows(load, store):
        @pl.loop(0, HALF, unroll=8)
        def _(t):
            turn[pl.ds(pl.multiple_of(t * 16, 16), 16), :] = load(t)

        for k in range(8):
            store(
                k,
                merge(turn[pl.ds(k, HALF, stride=16), :], turn[pl.ds(8 + k, HALF, stride=16), :]),
            )

    def turn_corner(load, store):
        for k in range(8):
            turn[pl.ds(k * 16, 16), :] = load(k)
        for k in range(8):
            store(k, merge(turn[pl.ds(k, 8, stride=16), :], turn[pl.ds(8 + k, 8, stride=16), :]))

    def pack_forward(index):
        @pl.loop(0, 8, unroll=8)
        def _(k):
            send_a[index, k] = pick(
                swap(frame[32 + k, CENTRE, :]), frame[40 + k, CENTRE, :]
            ).astype(BF16)
            send_b[index, k] = pick(
                frame[16 + k, CENTRE, :], swap(frame[24 + k, CENTRE, :])
            ).astype(BF16)

        @pl.loop(0, HALF, unroll=8)
        def _(t):
            send_l[index, t] = frame[16 + t, slice(64, 80), :].astype(BF16)
            send_r[index, t] = frame[16 + t, slice(16, 32), :].astype(BF16)

    def unpack_forward(index):
        def put_down_left(k, value):
            recv_c[index, FAR_BELOW - 4, k] = value.astype(BF16)

        @pl.when(off == 0)
        def _():
            def put_left(t, value):
                recv_l[index, t] = value.astype(BF16)

            def put_below(k, value):
                recv_b[index, k] = value.astype(BF16)

            rows_to_cols(lambda k: recv_a[index, k].astype(F32), put_left)
            cols_to_rows(lambda t: recv_r[index, t].astype(F32), put_below)
            turn_corner(
                lambda k: recv_c[index, FAR_ABOVE - 4, k].astype(F32), put_down_left
            )

        @pl.when(off == 1)
        def _():
            turn_corner(
                lambda k: send_a[index, k, first, :].astype(F32), put_down_left
            )

        @pl.loop(0, HALF, unroll=8)
        def _(t):
            frame[16 + t, EDGE_LOW, :] = recv_l[index, t].astype(F32)
            frame[16 + t, EDGE_HIGH, :] = recv_r[index, t].astype(F32)

        @pl.loop(0, 8, unroll=8)
        def _(k):
            above, below = (
                jnp.concatenate(
                    [recv_c[index, low - 4, k], strip[index, k], recv_c[index, high - 4, k]], axis=0
                ).astype(F32)
                for low, strip, high in (
                    (CORNER_ABOVE, recv_a, FAR_ABOVE),
                    (FAR_BELOW, recv_b, CORNER_BELOW),
                )
            )
            frame[k] = pick(above, swap(frame[32 + k]))
            frame[8 + k] = swap(pick(frame[40 + k], above))
            frame[48 + k] = swap(pick(below, frame[16 + k]))
            frame[56 + k] = pick(swap(frame[24 + k]), below)

    def prepare_weights(layer):
        weight = weight_ref[layer].astype(F32)
        pieces = [weight[:, j * LANES : (j + 1) * LANES] for j in range(4)]
        pieces.append(
            jnp.concatenate([weight[:, 512:576], jnp.zeros((CH, CH), F32)], axis=1)
        )
        turned = [jnp.concatenate([piece, piece], axis=0).T for piece in pieces]
        for a in range(3):
            for b in range(3):
                for pair, tap in enumerate((3 * a + b, 3 * b + a)):
                    plain = turned[tap // 2][(tap % 2) * CH : (tap % 2) * CH + CH]
                    low = is_low(plain.shape)
                    at = (3 * a + b) * LANES
                    lane = pair * LANES
                    w_fwd[layer, at : at + CH, lane : lane + LANES] = jnp.where(
                        low, plain, 0.0
                    ).astype(BF16)
                    w_fwd[layer, at + CH : at + LANES, lane : lane + LANES] = jnp.where(
                        low, 0.0, plain
                    ).astype(BF16)
                    own = pieces[tap // 2]
                    other = swap(own)
                    if tap % 2:
                        own, other = other, own
                    at = a * 2 * LANES + pair * LANES
                    lane = b * LANES
                    w_bwd[layer, at : at + CH, lane : lane + LANES] = jnp.where(
                        low, own, 0.0
                    ).astype(BF16)
                    w_bwd[layer, at + CH : at + LANES, lane : lane + LANES] = jnp.where(
                        low, 0.0, other
                    ).astype(BF16)

    def shift_columns(layer):
        spread = dilation_ref[layer]

        @pl.loop(0, 64, unroll=4)
        def _(t):
            for b in range(3):
                cols[layer, t, :, b * LANES : (b + 1) * LANES] = frame[
                    t, pl.ds(DMAX + (b - 1) * spread, BLOCK), :
                ].astype(BF16)

    def taps(layer, t, tiles):
        spread = dilation_ref[layer]
        return [
            cols[layer, pl.ds(DMAX + t + (a - 1) * spread, tiles)].reshape(tiles * BLOCK, 3 * LANES)
            for a in range(3)
        ]

    FWD = 8

    def forward(layer):
        bias = bias_ref[layer : layer + 1, :]
        bias = jnp.concatenate([bias, bias, bias, bias], axis=1)

        @pl.loop(0, HALF // FWD, unroll=4)
        def _(step):
            t = step * FWD
            mixed = (
                jnp.dot(
                    jnp.concatenate(taps(layer, t, FWD), axis=1),
                    w_fwd[layer],
                    preferred_element_type=F32,
                )
                + bias
            )
            value, slope = both_gelu(mixed)
            slopes[layer, pl.ds(t, FWD)] = slope.reshape(FWD, BLOCK, 2 * LANES)
            active = 0.5 * (value[:, :LANES] + value[:, LANES:])
            stored = frame[pl.ds(16 + t, FWD), CENTRE, :].reshape(FWD * BLOCK, LANES)
            result = (kept * (stored + active)).astype(BF16).astype(F32)
            result = result.reshape(FWD, BLOCK, LANES)
            if layer == LAYERS - 1:
                out_ref[pl.ds(t, FWD)] = result.astype(BF16)
            else:
                frame[pl.ds(16 + t, FWD), CENTRE, :] = result

    @pl.loop(0, 16, unroll=4)
    def _(k):
        tiles = (to_tiles(input_ref, k) * kept).astype(BF16).astype(F32)
        frame[16 + 2 * k, CENTRE, :] = tiles[:BLOCK]
        frame[17 + 2 * k, CENTRE, :] = tiles[BLOCK:]

    pack_forward(0)
    pl.semaphore_wait(barrier, count)
    send(0, range(8))
    for layer in range(LAYERS):
        prepare_weights(layer)

    @pl.loop(0, 16, unroll=4)
    def _(k):
        tiles = to_tiles(cot_ref, k)
        grad[2 * k] = tiles[:BLOCK]
        grad[2 * k + 1] = tiles[BLOCK:]

    for layer in range(LAYERS):
        wait(layer, range(8))
        unpack_forward(layer)
        shift_columns(layer)
        forward(layer)
        if layer < LAYERS - 1:
            pack_forward(layer + 1)
            send(layer + 1, range(8))

    @pl.loop(0, 16, unroll=4)
    def _(t):
        slope_low[t] = jnp.zeros((BLOCK, 2 * LANES), BF16)
        slope_low[48 + t] = jnp.zeros((BLOCK, 2 * LANES), BF16)

    @pl.loop(0, BWD, unroll=4)
    def _(t):
        for b in range(3):
            for slot in range(SLOTS):
                padded[slot, b, t, 0:32, :] = jnp.zeros((32, LANES), F32)
                padded[slot, b, t, 96:128, :] = jnp.zeros((32, LANES), F32)

    def slope_step(layer):
        def step(t, total):
            masked = kept * grad[t]
            grad[t] = masked
            half = 0.5 * masked
            slope = slopes[layer, t] * jnp.concatenate([half, half], axis=1)
            slope_low[16 + t] = slope.astype(BF16)
            return total + jnp.sum(slope.reshape(8, 8, 2 * LANES), axis=0)

        return lax.fori_loop(0, HALF, step, jnp.zeros((8, 2 * LANES), F32), unroll=4)

    def tile_grad(layer, steps):
        spread = dilation_ref[layer]

        def part(step, which, slot):
            first = step * BWD
            held = [
                slope_low[pl.ds(first - (a - 1) * spread, BWD)].reshape(BWD * BLOCK, 2 * LANES)
                for a in which
            ]
            left = held[0] if len(held) == 1 else jnp.concatenate(held, axis=1)
            rows = w_bwd[layer, which[0] * 2 * LANES : (which[-1] + 1) * 2 * LANES, :]
            result = jnp.dot(left, rows, preferred_element_type=F32)
            for b in range(3):
                padded[slot, b, :, 32:96, :] = result[:, b * LANES : (b + 1) * LANES].reshape(
                    BWD, BLOCK, LANES
                )
            for at in range(BWD):
                total = None
                for b in range(3):
                    term = padded[slot, b, at, pl.ds(DMAX - (b - 1) * spread, WIDE), :]
                    total = term if total is None else total + term
                frame[first + at] = total

        for count, step in enumerate(steps):
            at = step * BWD
            which = (0,) if at < 16 else (2,) if at >= 48 else (0, 1, 2)
            part(step, which, count % SLOTS)

    def pack_outer(index):
        @pl.loop(0, 8, unroll=8)
        def _(k):
            above[k] = pick(frame[k], swap(frame[8 + k]))
            below[k] = pick(swap(frame[48 + k]), frame[56 + k])

        @pl.when(off == 0)
        def _():
            def add_far(k, value):
                above[k, EDGE_HIGH, :] = above[k, EDGE_HIGH, :] + value

            turn_corner(lambda k: below[k, EDGE_LOW, :], add_far)

        @pl.loop(0, 8, unroll=8)
        def _(k):
            send_b[index, k] = below[k, CENTRE, :].astype(BF16)
            for piece, strip, part in (
                (CORNER_ABOVE, above, EDGE_LOW),
                (FAR_ABOVE, above, EDGE_HIGH),
                (FAR_BELOW, below, EDGE_LOW),
                (CORNER_BELOW, below, EDGE_HIGH),
            ):
                send_c[index - LAYERS, piece - 4, k] = strip[k, part, :].astype(BF16)

        @pl.when(off > 0)
        def _():
            send_above(index)

        send(index, (BELOW, CORNER_ABOVE, FAR_ABOVE, FAR_BELOW, CORNER_BELOW))

    def send_above(index):
        @pl.loop(0, 8, unroll=8)
        def _(k):
            send_a[index, k] = above[k, CENTRE, :].astype(BF16)

        send(index, (ABOVE,))

    def pack_centre(index):
        @pl.when(off == 0)
        def _():
            @pl.loop(0, 8, unroll=8)
            def _(k):
                share(k, EDGE_LOW)

            def add_above(k, value):
                above[k, CENTRE, :] = above[k, CENTRE, :] + value

            cols_to_rows(lambda t: frame[16 + t, EDGE_LOW, :], add_above)
            send_above(index)

            @pl.loop(0, 8, unroll=8)
            def _(k):
                share(k, slice(DMAX, WIDE))

            def add_right(t, value):
                frame[16 + t, EDGE_HIGH, :] = frame[16 + t, EDGE_HIGH, :] + value

            rows_to_cols(lambda k: below[k, CENTRE, :], add_right)

        @pl.when(off > 0)
        def _():
            @pl.loop(0, 8, unroll=8)
            def _(k):
                share(k, slice(0, WIDE))

        @pl.when(off == 1)
        def _():
            def add_own(k, value):
                low = is_low(value.shape)
                at = slice(16, 32)
                frame[32 + k, at, :] = frame[32 + k, at, :] + jnp.where(low, 0.0, swap(value))
                frame[40 + k, at, :] = frame[40 + k, at, :] + jnp.where(low, 0.0, value)

            turn_corner(lambda k: below[k, EDGE_LOW, :], add_own)

        @pl.loop(0, HALF, unroll=8)
        def _(t):
            send_l[index, t] = frame[16 + t, EDGE_LOW, :].astype(BF16)
            send_r[index, t] = frame[16 + t, EDGE_HIGH, :].astype(BF16)

        send(index, (LEFT, RIGHT))

    def share(k, part):
        def add(to, value, keep_low):
            low = is_low(value.shape)
            moved = swap(value)
            moved = jnp.where(low, moved, 0.0) if keep_low else jnp.where(low, 0.0, moved)
            frame[to, part, :] = frame[to, part, :] + moved

        add(16 + k, frame[48 + k, part, :], False)
        add(24 + k, frame[56 + k, part, :], False)
        add(32 + k, frame[k, part, :], True)
        add(40 + k, frame[8 + k, part, :], True)

    def unpack_backward(index):
        @pl.loop(0, HALF, unroll=8)
        def _(t):
            total = grad[t] + frame[16 + t, CENTRE, :]
            right = recv_r[index, t].astype(F32)
            left = recv_l[index, t].astype(F32)
            edge = jnp.concatenate([right, jnp.zeros((32, LANES), F32), left], axis=0)
            grad[t] = total + edge

        @pl.loop(0, 8, unroll=8)
        def _(k):
            def strip(ref, low, high):
                corners = [
                    recv_c[index, high - 4, k].astype(F32),
                    jnp.zeros((32, LANES), F32),
                    recv_c[index, low - 4, k].astype(F32),
                ]
                return ref[index, k].astype(F32) + jnp.concatenate(corners, axis=0)

            top = strip(recv_b, FAR_BELOW, CORNER_BELOW)
            bottom = strip(recv_a, CORNER_ABOVE, FAR_ABOVE)
            low = is_low(top.shape)
            grad[k] = grad[k] + jnp.where(low, top, 0.0)
            grad[8 + k] = grad[8 + k] + jnp.where(low, swap(top), 0.0)
            grad[16 + k] = grad[16 + k] + jnp.where(low, 0.0, swap(bottom))
            grad[24 + k] = grad[24 + k] + jnp.where(low, 0.0, bottom)

    PG = 16

    def weight_terms(layer, bias_rows):
        pair_grad[...] = jnp.zeros_like(pair_grad)

        @pl.loop(0, HALF // PG)
        def _(step):
            t = step * PG
            left = slope_low[pl.ds(16 + t, PG)].reshape(PG * BLOCK, 2 * LANES)
            for a, part in enumerate(taps(layer, t, PG)):
                lane = a * 3 * LANES
                pair_grad[:, lane : lane + 3 * LANES] += lax.dot_general(
                    left, part, (((0,), (0,)), ((), ())), preferred_element_type=F32
                )

        def tap_part(tap, half):
            turned = 3 * (tap % 3) + tap // 3
            first = pair_grad[half * CH : half * CH + CH, tap * LANES : (tap + 1) * LANES]
            at = LANES + half * CH
            second = pair_grad[at : at + CH, turned * LANES : (turned + 1) * LANES]
            return first + second

        for j in range(5):
            low_part = tap_part(2 * j, 0) + swap(tap_part(2 * j, 1))
            if j < 4:
                high_part = tap_part(2 * j + 1, 1) + swap(tap_part(2 * j + 1, 0))
            else:
                total = jnp.sum(bias_rows, axis=0, keepdims=True)
                total = total[:, :LANES] + total[:, LANES:]
                total = total + swap(total)
                high_part = jnp.broadcast_to(total, (LANES, LANES)).T[:CH]
            part = pick(low_part, high_part).astype(BF16)
            for at in range(CH // rows):
                term_ref[layer * (CH // rows) + at, :, j * LANES : (j + 1) * LANES] = part[
                    at * rows : (at + 1) * rows
                ]

    def sum_copy(stage, step):
        if stage == 1:
            other, device = across(step)
            source, target = shards.at[mine], shards.at[mine]
        else:
            other, device = in_plane(step)
            if stage == 0:
                source, target = term_ref.at[other], slots.at[step]
            else:
                source, target = whole.at[inner], whole.at[inner]
        return pltpu.make_async_remote_copy(
            src_ref=source,
            dst_ref=target,
            send_sem=sum_send.at[stage, step],
            recv_sem=sum_recv.at[stage, step],
            device_id=device,
            device_id_type=MESH,
        )

    def peers(stage):
        return range(1, many if stage == 1 else group)

    def sum_start(stage):
        if stage == 1:
            total = term_ref[inner].astype(F32)
            for step in peers(0):
                sum_copy(0, step).wait_recv()
                total = total + slots[step].astype(F32)
            shards[mine] = total
        elif stage == 2:
            for step in peers(1):
                sum_copy(1, step).wait_recv()
            total = shards[0]
            for at in range(1, many):
                total = total + shards[at]
            whole[inner] = (total * scale).astype(BF16)
        for step in peers(stage):
            sum_copy(stage, step).start()

    def sum_end():
        for step in peers(2):
            sum_copy(2, step).wait_recv()
        sums_ref[...] = whole[...].astype(F32)
        for stage in range(3):
            for step in peers(stage):
                sum_copy(stage, step).wait_send()

    for layer in reversed(range(LAYERS)):
        index = 2 * LAYERS - 1 - layer
        bias_rows = slope_step(layer)
        if layer == 0:
            weight_terms(layer, bias_rows)
            sum_start(0)
        edge = 64 // BWD // 4
        tile_grad(layer, (*range(edge), *range(3 * edge, 4 * edge)))
        pack_outer(index)
        tile_grad(layer, range(edge, 3 * edge))
        pack_centre(index)
        if layer == 0:
            sum_start(1)
            sum_start(2)
        else:
            weight_terms(layer, bias_rows)
        wait(index, range(8))
        unpack_backward(index)

    @pl.loop(0, HALF, unroll=4)
    def _(t):
        grad_ref[t] = kept * grad[t]

    sum_end()
    for index in range(2 * LAYERS):
        finish(index)


def finish_kernel(
    tiles_ref, grad_ref, sums_ref, out_ref, grad_out_ref, weight_ref, bias_ref, tiles, grad, out, turned, sems
):
    parts = 4
    each = HALF // parts
    lanes = each * BLOCK
    half = HALF * BLOCK
    loads = []
    for part in range(parts):
        span = pl.ds(part * each, each)
        loads.append(
            (
                pltpu.make_async_copy(tiles_ref.at[span], tiles.at[span], sems.at[0, part]),
                pltpu.make_async_copy(grad_ref.at[span], grad.at[span], sems.at[1, part]),
            )
        )
        for copy in loads[-1]:
            copy.start()
    total = jnp.concatenate([sums_ref[at] for at in range(sums_ref.shape[0])], axis=0)
    for layer in range(LAYERS):
        weight_ref[layer] = total[layer * CH : (layer + 1) * CH, :576]
    column = total[:, 4 * LANES :].T[CH : CH + 1]
    bias_ref[0:1, :] = column[:, :CH]
    bias_ref[1:2, :] = swap(column)[:, :CH]
    stores = []
    for part in range(parts):
        for at, (source, held, target) in enumerate(((tiles, out, out_ref), (grad, turned, grad_out_ref))):
            loads[part][at].wait()
            for k in range(part * each // 2, (part + 1) * each // 2):
                both = source[2 * k : 2 * k + 2].reshape(LANES, LANES).astype(F32).T
                both = both.astype(held.dtype)
                held[:, k * LANES : (k + 1) * LANES] = both[:CH]
                held[:, half + k * LANES : half + (k + 1) * LANES] = both[CH:]
            for side in range(2):
                span = pl.ds(side * half + part * lanes, lanes)
                copy = pltpu.make_async_copy(
                    held.at[:, span], target.at[:, span], sems.at[2 + 2 * at + side, part]
                )
                copy.start()
                stores.append(copy)
    for copy in stores:
        copy.wait()


def per_device(input_map, cotangent, band_width, dilation, conv_weight, conv_bias):
    rows_all = lax.axis_size("pos")
    offsets_all = lax.axis_size("band")
    bins = BLOCK * BLOCK
    vmem = pl.BlockSpec(memory_space=pltpu.VMEM)
    smem = pl.BlockSpec(memory_space=pltpu.SMEM)
    group = 16 if rows_all % 16 == 0 else rows_all
    many = rows_all // group * offsets_all
    shard = (LAYERS * CH // group, 5 * LANES)
    scale = 1.0 / (BLOCK * math.sqrt(input_map.shape[0] * rows_all * offsets_all))
    tiles, grad, sums = pl.pallas_call(
        functools.partial(net_kernel, rows_all, offsets_all, scale),
        out_shape=(
            jax.ShapeDtypeStruct((HALF, BLOCK, LANES), BF16),
            jax.ShapeDtypeStruct((HALF, BLOCK, LANES), F32),
            jax.ShapeDtypeStruct((group, *shard), F32),
        ),
        in_specs=[smem, smem, vmem, vmem, vmem, vmem],
        out_specs=(vmem, vmem, vmem),
        scratch_shapes=[
            pltpu.VMEM((64, WIDE, LANES), F32),
            pltpu.VMEM((group, *shard), BF16),
            pltpu.VMEM((group, *shard), BF16),
            pltpu.VMEM((many, *shard), F32),
            pltpu.VMEM((group, *shard), BF16),
            pltpu.VMEM((LAYERS, 64, BLOCK, 3 * LANES), BF16),
            pltpu.VMEM((LAYERS, HALF, BLOCK, 2 * LANES), F32),
            pltpu.VMEM((64, BLOCK, 2 * LANES), BF16),
            pltpu.VMEM((SLOTS, 3, BWD, 128, LANES), F32),
            pltpu.VMEM((HALF, BLOCK, LANES), F32),
            pltpu.VMEM((8, WIDE, LANES), F32),
            pltpu.VMEM((8, WIDE, LANES), F32),
            pltpu.VMEM((2 * LANES, 9 * LANES), F32),
            pltpu.VMEM((LAYERS, 9 * LANES, 2 * LANES), BF16),
            pltpu.VMEM((LAYERS, 6 * LANES, 3 * LANES), BF16),
            pltpu.VMEM((512, LANES), F32),
            pltpu.VMEM((4, 8, BLOCK, LANES), BF16),
            pltpu.VMEM((4, 8, BLOCK, LANES), BF16),
            pltpu.VMEM((4, HALF, DMAX, LANES), BF16),
            pltpu.VMEM((4, HALF, DMAX, LANES), BF16),
            pltpu.VMEM((2, 4, 8, DMAX, LANES), BF16),
            pltpu.VMEM((4, 8, BLOCK, LANES), BF16),
            pltpu.VMEM((4, 8, BLOCK, LANES), BF16),
            pltpu.VMEM((4, HALF, DMAX, LANES), BF16),
            pltpu.VMEM((4, HALF, DMAX, LANES), BF16),
            pltpu.VMEM((4, 4, 8, DMAX, LANES), BF16),
            pltpu.SemaphoreType.DMA((4, 8)),
            pltpu.SemaphoreType.DMA((4, 8)),
            pltpu.SemaphoreType.DMA((3, 16)),
            pltpu.SemaphoreType.DMA((3, 16)),
        ],
        compiler_params=pltpu.CompilerParams(collective_id=0, has_side_effects=True),
        name="net",
    )(
        band_width,
        dilation,
        input_map.reshape(CH, bins),
        cotangent.reshape(CH, bins),
        conv_weight,
        conv_bias,
    )
    anywhere = pl.BlockSpec(memory_space=pl.ANY)
    output, input_grad, weight_grad, bias_grad = pl.pallas_call(
        finish_kernel,
        out_shape=(
            jax.ShapeDtypeStruct((CH, bins), BF16),
            jax.ShapeDtypeStruct((CH, bins), F32),
            jax.ShapeDtypeStruct((LAYERS, CH, 576), F32),
            jax.ShapeDtypeStruct((LAYERS, CH), F32),
        ),
        in_specs=[anywhere, anywhere, vmem],
        out_specs=(anywhere, anywhere, vmem, vmem),
        scratch_shapes=[
            pltpu.VMEM((HALF, BLOCK, LANES), BF16),
            pltpu.VMEM((HALF, BLOCK, LANES), F32),
            pltpu.VMEM((CH, bins), BF16),
            pltpu.VMEM((CH, bins), F32),
            pltpu.SemaphoreType.DMA((6, 4)),
        ],
        name="finish",
    )(tiles, grad, sums)
    return (
        output.reshape(input_map.shape),
        input_grad.reshape(input_map.shape),
        weight_grad,
        bias_grad,
    )


def solution(mesh):
    split = P(None, "pos", "band", None, None)
    return jax.shard_map(
        per_device,
        mesh=mesh,
        in_specs=(split, split, P("pos"), P(), P(), P()),
        out_specs=(split, split, P(), P()),
        check_vma=False,
    )
```

profile of v0, /device:TPU:1, one launch (start us, length us, event | category | flops | bytes accessed | tf_op | source)
XLA Modules:
  0.0 69.8 jit_solution(13890028773984143906)
XLA Ops:
  1.3 63.9 %net.1 = (bf16[32,64,128]{2,1,0:T(8,128)(2,1)}, f32[32,64,128]{2,1,0:T(8,128)}, f32[16,8,640]{2,1,0:T(8,128)}) custom-call(s32[1]{0:T(128)S(6)} %copy.10.width_ref, s32[2]{0:T(128)} %dilation_ref.1, bf16[64,4096]{1,0:T(8,128)(2,1)} %bitcast.4, bf16[64,4096]{1,0:T(8,128)(2,1)} %bitcast.5, bf16[2,64,576]{2,1,0:T(8,128)(2,1)} %weight_ref.1, f32[2,64]{1,0:T(2,128)} %bias_ref.1), custom_call_target="tpu_custom_call" | custom-call | tf_op jit(solution)/shard_map/net/pallas_call | solution.py:759
  65.1 4.5 %finish.1 = (bf16[64,4096]{1,0:T(8,128)(2,1)}, f32[64,4096]{1,0:T(8,128)}, f32[2,64,576]{2,1,0:T(8,128)}, f32[2,64]{1,0:T(2,128)}) custom-call(bf16[32,64,128]{2,1,0:T(8,128)(2,1)} %get-tuple-element.11.tiles_ref, f32[32,64,128]{2,1,0:T(8,128)} %get-tuple-element.12.grad_ref, f32[16,8,640]{2,1,0:T(8,128)} %get-tuple-element.13.sums_ref), custom_call_target="tpu_custom_call" | custom-call | tf_op jit(solution)/shard_map/finish/pallas_call | solution.py:811
where the time goes:
time: 70 us; the launch traced here: 69.8 us
  Pallas kernels  68.4 us (98%)
  between operations  1.45 us (2%)
    pallas_call x1, Pallas kernels, per_device(): pl.pallas_call(functools.partial(net_kernel, rows_all, offsets_all, scale...  63.9 us
    pallas_call x1, Pallas kernels, per_device(): pl.pallas_call(finish_kernel, out_shape=(jax.ShapeDtypeStruct((CH, bins),...  4.5 us

commit v1 on v0

--- a/solution.py
+++ b/solution.py
@@ -67,8 +67,10 @@
     bias_ref,
     out_ref,
     grad_ref,
-    sums_ref,
+    weight_grad_ref,
+    bias_grad_ref,
     frame,
+    last,
     term_ref,
     slots,
     shards,
@@ -228,6 +230,11 @@
         second = source[:, pl.ds(pl.multiple_of((k + 16) * LANES, LANES), LANES)].astype(F32)
         return jnp.concatenate([first, second], axis=0).T
 
+    def from_tiles(target, k, first, second):
+        turned = jnp.concatenate([first, second], axis=0).T.astype(target.dtype)
+        target[:, pl.ds(pl.multiple_of(k * LANES, LANES), LANES)] = turned[:CH]
+        target[:, pl.ds(pl.multiple_of((k + 16) * LANES, LANES), LANES)] = turned[CH:]
+
     def rows_to_cols(load, store):
         @pl.loop(0, 8, unroll=8)
         def _(k):
@@ -387,7 +394,7 @@
             result = (kept * (stored + active)).astype(BF16).astype(F32)
             result = result.reshape(FWD, BLOCK, LANES)
             if layer == LAYERS - 1:
-                out_ref[pl.ds(t, FWD)] = result.astype(BF16)
+                last[pl.ds(t, FWD)] = result
             else:
                 frame[pl.ds(16 + t, FWD), CENTRE, :] = result
 
@@ -590,20 +597,13 @@
             grad[16 + k] = grad[16 + k] + jnp.where(low, 0.0, swap(bottom))
             grad[24 + k] = grad[24 + k] + jnp.where(low, 0.0, bottom)
 
-    PG = 16
-
     def weight_terms(layer, bias_rows):
-        pair_grad[...] = jnp.zeros_like(pair_grad)
-
-        @pl.loop(0, HALF // PG)
-        def _(step):
-            t = step * PG
-            left = slope_low[pl.ds(16 + t, PG)].reshape(PG * BLOCK, 2 * LANES)
-            for a, part in enumerate(taps(layer, t, PG)):
-                lane = a * 3 * LANES
-                pair_grad[:, lane : lane + 3 * LANES] += lax.dot_general(
-                    left, part, (((0,), (0,)), ((), ())), preferred_element_type=F32
-                )
+        left = slope_low[16:48].reshape(HALF * BLOCK, 2 * LANES)
+        for a, part in enumerate(taps(layer, 0, HALF)):
+            lane = a * 3 * LANES
+            pair_grad[:, lane : lane + 3 * LANES] = lax.dot_general(
+                left, part, (((0,), (0,)), ((), ())), preferred_element_type=F32
+            )
 
         def tap_part(tap, half):
             turned = 3 * (tap % 3) + tap // 3
@@ -669,7 +669,12 @@
     def sum_end():
         for step in peers(2):
             sum_copy(2, step).wait_recv()
-        sums_ref[...] = whole[...].astype(F32)
+        total = jnp.concatenate([whole[at].astype(F32) for at in range(group)], axis=0)
+        for layer in range(LAYERS):
+            weight_grad_ref[layer] = total[layer * CH : (layer + 1) * CH, :576]
+        column = total[:, 4 * LANES :].T[CH : CH + 1]
+        bias_grad_ref[0:1, :] = column[:, :CH]
+        bias_grad_ref[1:2, :] = swap(column)[:, :CH]
         for stage in range(3):
             for step in peers(stage):
                 sum_copy(stage, step).wait_send()
@@ -690,59 +695,38 @@
             sum_start(2)
         else:
             weight_terms(layer, bias_rows)
+
+            @pl.loop(0, 16, unroll=4)
+            def _(k):
+                from_tiles(out_ref, k, last[2 * k], last[2 * k + 1])
+
         wait(index, range(8))
         unpack_backward(index)
 
-    @pl.loop(0, HALF, unroll=4)
-    def _(t):
-        grad_ref[t] = kept * grad[t]
+    @pl.loop(0, 16, unroll=4)
+    def _(k):
+        from_tiles(grad_ref, k, kept * grad[2 * k], kept * grad[2 * k + 1])
 
     sum_end()
     for index in range(2 * LAYERS):
         finish(index)
 
 
-def finish_kernel(
-    tiles_ref, grad_ref, sums_ref, out_ref, grad_out_ref, weight_ref, bias_ref, tiles, grad, out, turned, sems
-):
-    parts = 4
-    each = HALF // parts
-    lanes = each * BLOCK
-    half = HALF * BLOCK
-    loads = []
-    for part in range(parts):
-        span = pl.ds(part * each, each)
-        loads.append(
-            (
-                pltpu.make_async_copy(tiles_ref.at[span], tiles.at[span], sems.at[0, part]),
-                pltpu.make_async_copy(grad_ref.at[span], grad.at[span], sems.at[1, part]),
-            )
-        )
-        for copy in loads[-1]:
-            copy.start()
-    total = jnp.concatenate([sums_ref[at] for at in range(sums_ref.shape[0])], axis=0)
-    for layer in range(LAYERS):
-        weight_ref[layer] = total[layer * CH : (layer + 1) * CH, :576]
-    column = total[:, 4 * LANES :].T[CH : CH + 1]
-    bias_ref[0:1, :] = column[:, :CH]
-    bias_ref[1:2, :] = swap(column)[:, :CH]
-    stores = []
-    for part in range(parts):
-        for at, (source, held, target) in enumerate(((tiles, out, out_ref), (grad, turned, grad_out_ref))):
-            loads[part][at].wait()
-            for k in range(part * each // 2, (part + 1) * each // 2):
-                both = source[2 * k : 2 * k + 2].reshape(LANES, LANES).astype(F32).T
-                both = both.astype(held.dtype)
-                held[:, k * LANES : (k + 1) * LANES] = both[:CH]
-                held[:, half + k * LANES : half + (k + 1) * LANES] = both[CH:]
-            for side in range(2):
-                span = pl.ds(side * half + part * lanes, lanes)
-                copy = pltpu.make_async_copy(
-                    held.at[:, span], target.at[:, span], sems.at[2 + 2 * at + side, part]
-                )
-                copy.start()
-                stores.append(copy)
-    for copy in stores:
+def finish_kernel(*refs):
+    sources, targets, sems = refs[:4], refs[4:8], refs[8]
+    copies = []
+    for at, (source, target) in enumerate(zip(sources, targets)):
+        parts = 4 if at < 2 else 1
+        for part in range(parts):
+            if parts > 1:
+                lanes = source.shape[1] // parts
+                span = pl.ds(part * lanes, lanes)
+                pair = source.at[:, span], target.at[:, span]
+            else:
+                pair = source, target
+            copies.append(pltpu.make_async_copy(*pair, sems.at[at, part]))
+            copies[-1].start()
+    for copy in copies:
         copy.wait()
 
 
@@ -756,17 +740,20 @@
     many = rows_all // group * offsets_all
     shard = (LAYERS * CH // group, 5 * LANES)
     scale = 1.0 / (BLOCK * math.sqrt(input_map.shape[0] * rows_all * offsets_all))
-    tiles, grad, sums = pl.pallas_call(
+    shapes = (
+        jax.ShapeDtypeStruct((CH, bins), BF16),
+        jax.ShapeDtypeStruct((CH, bins), F32),
+        jax.ShapeDtypeStruct((LAYERS, CH, 576), F32),
+        jax.ShapeDtypeStruct((LAYERS, CH), F32),
+    )
+    results = pl.pallas_call(
         functools.partial(net_kernel, rows_all, offsets_all, scale),
-        out_shape=(
-            jax.ShapeDtypeStruct((HALF, BLOCK, LANES), BF16),
-            jax.ShapeDtypeStruct((HALF, BLOCK, LANES), F32),
-            jax.ShapeDtypeStruct((group, *shard), F32),
-        ),
+        out_shape=shapes,
         in_specs=[smem, smem, vmem, vmem, vmem, vmem],
-        out_specs=(vmem, vmem, vmem),
+        out_specs=(vmem, vmem, vmem, vmem),
         scratch_shapes=[
             pltpu.VMEM((64, WIDE, LANES), F32),
+            pltpu.VMEM((HALF, BLOCK, LANES), F32),
             pltpu.VMEM((group, *shard), BF16),
             pltpu.VMEM((group, *shard), BF16),
             pltpu.VMEM((many, *shard), F32),
@@ -797,7 +784,9 @@
             pltpu.SemaphoreType.DMA((3, 16)),
             pltpu.SemaphoreType.DMA((3, 16)),
         ],
-        compiler_params=pltpu.CompilerParams(collective_id=0, has_side_effects=True),
+        compiler_params=pltpu.CompilerParams(
+            collective_id=0, has_side_effects=True, vmem_limit_bytes=46 * 2**20
+        ),
         name="net",
     )(
         band_width,
@@ -810,23 +799,13 @@
     anywhere = pl.BlockSpec(memory_space=pl.ANY)
     output, input_grad, weight_grad, bias_grad = pl.pallas_call(
         finish_kernel,
-        out_shape=(
-            jax.ShapeDtypeStruct((CH, bins), BF16),
-            jax.ShapeDtypeStruct((CH, bins), F32),
-            jax.ShapeDtypeStruct((LAYERS, CH, 576), F32),
-            jax.ShapeDtypeStruct((LAYERS, CH), F32),
-        ),
-        in_specs=[anywhere, anywhere, vmem],
-        out_specs=(anywhere, anywhere, vmem, vmem),
-        scratch_shapes=[
-            pltpu.VMEM((HALF, BLOCK, LANES), BF16),
-            pltpu.VMEM((HALF, BLOCK, LANES), F32),
-            pltpu.VMEM((CH, bins), BF16),
-            pltpu.VMEM((CH, bins), F32),
-            pltpu.SemaphoreType.DMA((6, 4)),
-        ],
+        out_shape=shapes,
+        in_specs=[vmem] * 4,
+        out_specs=(anywhere,) * 4,
+        scratch_shapes=[pltpu.SemaphoreType.DMA((4, 4))],
+        compiler_params=pltpu.CompilerParams(vmem_limit_bytes=4 * 2**20),
         name="finish",
-    )(tiles, grad, sums)
+    )(*results)
     return (
         output.reshape(input_map.shape),
         input_grad.reshape(input_map.shape),

time: 70 us -> 68.5 us (0.979)
  Pallas kernels: 68.4 us -> 63.1 us
  local copies, waits for them, and re-layouts: 0 us -> 3.66 us
    unnamed x0 -> x10, local copies, waits for them, and re-layouts: none -> 3.66 us
    pallas_call x1, Pallas kernels: 4.5 us -> 1.39 us  [per_device(): pl.pallas_call(finish_kernel, out_shape=shapes, in_specs=[vmem] * 4, out_...]
    pallas_call x1, Pallas kernels: 63.9 us -> 61.7 us  [per_device(): pl.pallas_call(functools.partial(net_kernel, rows_all, offsets_all, scale...]
where the time goes in v1:
time: 68.5 us; the launch traced here: 68.2 us
  Pallas kernels  63.1 us (92%)
  local copies, waits for them, and re-layouts  3.66 us (5%)
  between operations  1.47 us (2%)
    pallas_call x1, Pallas kernels, per_device(): pl.pallas_call(functools.partial(net_kernel, rows_all, offsets_all, scale...  61.7 us
    unnamed x10, local copies, waits for them, and re-layouts  3.66 us
    pallas_call x1, Pallas kernels, per_device(): pl.pallas_call(finish_kernel, out_shape=shapes, in_specs=[vmem] * 4, out_...  1.39 us

profile of v1, /device:TPU:1, one launch (start us, length us, event | category | flops | bytes accessed | tf_op | source)
XLA Modules:
  0.0 68.2 jit_solution(15080537686131380487)
XLA Ops:
  1.3 0.0 copy-start.3
  1.3 0.0 copy-start.4
  1.3 0.7 copy-done.3
  2.0 0.0 copy-done.4
  2.0 0.0 copy-start
  2.0 1.0 %copy-done = bf16[1,1,1,64,4096]{4,3,2,1,0:T(8,128)(2,1)S(1)} copy-done((bf16[1,1,1,64,4096]{4,3,2,1,0:T(8,128)(2,1)S(1)}, bf16[1,1,1,64,4096]{4,3,2,1,0:T(8,128)(2,1)}, u32[]{:S(2)}) %copy-start) | copy-done | bytes 524312
  3.0 0.0 copy-start.1
  3.0 1.0 %copy-done.1 = bf16[1,1,1,64,4096]{4,3,2,1,0:T(8,128)(2,1)S(1)} copy-done((bf16[1,1,1,64,4096]{4,3,2,1,0:T(8,128)(2,1)S(1)}, bf16[1,1,1,64,4096]{4,3,2,1,0:T(8,128)(2,1)}, u32[]{:S(2)}) %copy-start.1) | copy-done | bytes 524312
  4.0 0.0 copy-start.2
  4.0 0.9 %copy-done.2 = bf16[2,64,576]{2,1,0:T(8,128)(2,1)S(1)} copy-done((bf16[2,64,576]{2,1,0:T(8,128)(2,1)S(1)}, bf16[2,64,576]{2,1,0:T(8,128)(2,1)}, u32[]{:S(2)}) %copy-start.2) | copy-done | bytes 147480
  5.0 61.7 %net.1 = (bf16[64,4096]{1,0:T(8,128)(2,1)S(1)}, f32[64,4096]{1,0:T(8,128)S(1)}, f32[2,64,576]{2,1,0:T(8,128)S(1)}, f32[2,64]{1,0:T(2,128)S(1)}) custom-call(s32[1]{0:T(128)S(6)} %copy.10.width_ref, s32[2]{0:T(128)S(1)} %copy-done.4, bf16[64,4096]{1,0:T(8,128)(2,1)S(1)} %bitcast.4, bf16[64,4096]{1,0:T(8,128)(2,1)S(1)} %bitcast.5, ...), custom_call_target="tpu_custom_call" | custom-call | tf_op jit(solution)/shard_map/net/pallas_call | solution.py:749
  66.7 1.4 %finish.1 = (bf16[64,4096]{1,0:T(8,128)(2,1)}, f32[64,4096]{1,0:T(8,128)}, f32[2,64,576]{2,1,0:T(8,128)}, f32[2,64]{1,0:T(2,128)}) custom-call(bf16[64,4096]{1,0:T(8,128)(2,1)S(1)} %get-tuple-element.12.refs_0_, f32[64,4096]{1,0:T(8,128)S(1)} %get-tuple-element.13.refs_1_, f32[2,64,576]{2,1,0:T(8,128)S(1)} %get-tuple-element.14.refs_2_, ...), custom_call_target="tpu_custom_call" | custom-call | tf_op jit(solution)/shard_map/finish/pallas_call | solution.py:800
Async XLA Ops:
  1.3 0.7 copy-start.3
  1.3 0.7 copy-start.4
  2.0 1.0 %copy-start = (bf16[1,1,1,64,4096]{4,3,2,1,0:T(8,128)(2,1)S(1)}, bf16[1,1,1,64,4096]{4,3,2,1,0:T(8,128)(2,1)}, u32[]{:S(2)}) copy-start(bf16[1,1,1,64,4096]{4,3,2,1,0:T(8,128)(2,1)} %param.6) | copy-start | bytes 1572868
  3.0 1.0 %copy-start.1 = (bf16[1,1,1,64,4096]{4,3,2,1,0:T(8,128)(2,1)S(1)}, bf16[1,1,1,64,4096]{4,3,2,1,0:T(8,128)(2,1)}, u32[]{:S(2)}) copy-start(bf16[1,1,1,64,4096]{4,3,2,1,0:T(8,128)(2,1)} %param.7) | copy-start | bytes 1572868
  4.0 0.9 %copy-start.2 = (bf16[2,64,576]{2,1,0:T(8,128)(2,1)S(1)}, bf16[2,64,576]{2,1,0:T(8,128)(2,1)}, u32[]{:S(2)}) copy-start(bf16[2,64,576]{2,1,0:T(8,128)(2,1)} %weight_ref.1) | copy-start | bytes 442372

commit v2 on v1

--- a/solution.py
+++ b/solution.py
@@ -61,14 +61,19 @@
     scale,
     width_ref,
     dilation_ref,
+    input_hbm,
+    cot_hbm,
+    weight_hbm,
+    bias_hbm,
+    out_ref,
+    grad_ref,
+    weight_grad_ref,
+    bias_grad_ref,
     input_ref,
     cot_ref,
     weight_ref,
     bias_ref,
-    out_ref,
-    grad_ref,
-    weight_grad_ref,
-    bias_grad_ref,
+    load_sem,
     frame,
     last,
     term_ref,
@@ -103,6 +108,19 @@
 ):
     row = lax.axis_index("pos")
     off = lax.axis_index("band")
+    loads = [
+        pltpu.make_async_copy(source, target, load_sem.at[at])
+        for at, (source, target) in enumerate(
+            (
+                (input_hbm, input_ref),
+                (weight_hbm, weight_ref),
+                (bias_hbm, bias_ref),
+                (cot_hbm, cot_ref),
+            )
+        )
+    ]
+    for load in loads:
+        load.start()
 
     def exists(di, do):
         return (row + di >= 0) & (row + di < rows_all) & (off + do >= 0) & (off + do < offsets_all)
@@ -398,6 +416,8 @@
             else:
                 frame[pl.ds(16 + t, FWD), CENTRE, :] = result
 
+    loads[0].wait()
+
     @pl.loop(0, 16, unroll=4)
     def _(k):
         tiles = (to_tiles(input_ref, k) * kept).astype(BF16).astype(F32)
@@ -407,8 +427,11 @@
     pack_forward(0)
     pl.semaphore_wait(barrier, count)
     send(0, range(8))
+    loads[1].wait()
+    loads[2].wait()
     for layer in range(LAYERS):
         prepare_weights(layer)
+    loads[3].wait()
 
     @pl.loop(0, 16, unroll=4)
     def _(k):
@@ -736,6 +759,7 @@
     bins = BLOCK * BLOCK
     vmem = pl.BlockSpec(memory_space=pltpu.VMEM)
     smem = pl.BlockSpec(memory_space=pltpu.SMEM)
+    hbm = pl.BlockSpec(memory_space=pltpu.HBM)
     group = 16 if rows_all % 16 == 0 else rows_all
     many = rows_all // group * offsets_all
     shard = (LAYERS * CH // group, 5 * LANES)
@@ -749,9 +773,14 @@
     results = pl.pallas_call(
         functools.partial(net_kernel, rows_all, offsets_all, scale),
         out_shape=shapes,
-        in_specs=[smem, smem, vmem, vmem, vmem, vmem],
+        in_specs=[smem, smem, hbm, hbm, hbm, hbm],
         out_specs=(vmem, vmem, vmem, vmem),
         scratch_shapes=[
+            pltpu.VMEM((CH, bins), BF16),
+            pltpu.VMEM((CH, bins), BF16),
+            pltpu.VMEM((LAYERS, CH, 576), BF16),
+            pltpu.VMEM((LAYERS, CH), F32),
+            pltpu.SemaphoreType.DMA((4,)),
             pltpu.VMEM((64, WIDE, LANES), F32),
             pltpu.VMEM((HALF, BLOCK, LANES), F32),
             pltpu.VMEM((group, *shard), BF16),
@@ -791,10 +820,10 @@
     )(
         band_width,
         dilation,
-        input_map.reshape(CH, bins),
-        cotangent.reshape(CH, bins),
-        conv_weight,
-        conv_bias,
+        pltpu.with_memory_space_constraint(input_map.reshape(CH, bins), pltpu.HBM),
+        pltpu.with_memory_space_constraint(cotangent.reshape(CH, bins), pltpu.HBM),
+        pltpu.with_memory_space_constraint(conv_weight, pltpu.HBM),
+        pltpu.with_memory_space_constraint(conv_bias, pltpu.HBM),
     )
     anywhere = pl.BlockSpec(memory_space=pl.ANY)
     output, input_grad, weight_grad, bias_grad = pl.pallas_call(

time: 68.5 us -> 65.4 us (0.955)
  local copies, waits for them, and re-layouts: 3.66 us -> 0.65 us
    unnamed x10 -> x2, local copies, waits for them, and re-layouts: 3.66 us -> 0.65 us
where the time goes in v2:
time: 65.4 us; the launch traced here: 65.2 us
  Pallas kernels  63.1 us (96%)
  between operations  1.45 us (2%)
    pallas_call x1, Pallas kernels, per_device(): pl.pallas_call(functools.partial(net_kernel, rows_all, offsets_all, scale...  61.7 us
    pallas_call x1, Pallas kernels, per_device(): pl.pallas_call(finish_kernel, out_shape=shapes, in_specs=[vmem] * 4, out_...  1.39 us

profile of v2, /device:TPU:1, one launch (start us, length us, event | category | flops | bytes accessed | tf_op | source)
XLA Modules:
  0.0 65.2 jit_solution(18038995310504695431)
XLA Ops:
  1.3 0.0 copy-start
  1.3 0.6 copy-done
  1.9 61.7 %net.1 = (bf16[64,4096]{1,0:T(8,128)(2,1)S(1)}, f32[64,4096]{1,0:T(8,128)S(1)}, f32[2,64,576]{2,1,0:T(8,128)S(1)}, f32[2,64]{1,0:T(2,128)S(1)}) custom-call(s32[1]{0:T(128)S(6)} %copy.10.width_ref, s32[2]{0:T(128)S(1)} %copy-done, bf16[64,4096]{1,0:T(8,128)(2,1)} %bitcast.4, bf16[64,4096]{1,0:T(8,128)(2,1)} %bitcast.5, bf16[2,64,576]{2,1,0:T(8,128)(2,1)} %weight_hbm.1, ...), custom_call_target="tpu_custom_call" | custom-call | tf_op jit(solution)/shard_map/net/pallas_call | solution.py:773
  63.7 1.4 %finish.1 = (bf16[64,4096]{1,0:T(8,128)(2,1)}, f32[64,4096]{1,0:T(8,128)}, f32[2,64,576]{2,1,0:T(8,128)}, f32[2,64]{1,0:T(2,128)}) custom-call(bf16[64,4096]{1,0:T(8,128)(2,1)S(1)} %get-tuple-element.12.refs_0_, f32[64,4096]{1,0:T(8,128)S(1)} %get-tuple-element.13.refs_1_, f32[2,64,576]{2,1,0:T(8,128)S(1)} %get-tuple-element.14.refs_2_, ...), custom_call_target="tpu_custom_call" | custom-call | tf_op jit(solution)/shard_map/finish/pallas_call | solution.py:829
Async XLA Ops:
  1.3 0.7 %copy-start = (s32[2]{0:T(128)S(1)}, s32[2]{0:T(128)}, u32[]{:S(2)}) copy-start(s32[2]{0:T(128)} %dilation_ref.1) | copy-start | bytes 28

commit v3 on v2

--- a/solution.py
+++ b/solution.py
@@ -293,34 +293,45 @@
             send_l[index, t] = frame[16 + t, slice(64, 80), :].astype(BF16)
             send_r[index, t] = frame[16 + t, slice(16, 32), :].astype(BF16)
 
-    def unpack_forward(index):
-        def put_down_left(k, value):
-            recv_c[index, FAR_BELOW - 4, k] = value.astype(BF16)
-
+    def unpack_sides(index):
         @pl.when(off == 0)
         def _():
-            def put_left(t, value):
-                recv_l[index, t] = value.astype(BF16)
-
             def put_below(k, value):
                 recv_b[index, k] = value.astype(BF16)
 
-            rows_to_cols(lambda k: recv_a[index, k].astype(F32), put_left)
             cols_to_rows(lambda t: recv_r[index, t].astype(F32), put_below)
+
+        @pl.when(off == 1)
+        def _():
             turn_corner(
-                lambda k: recv_c[index, FAR_ABOVE - 4, k].astype(F32), put_down_left
+                lambda k: send_a[index, k, first, :].astype(F32),
+                functools.partial(put_down_left, index),
             )
 
-        @pl.when(off == 1)
-        def _():
-            turn_corner(
-                lambda k: send_a[index, k, first, :].astype(F32), put_down_left
-            )
+        @pl.when(off > 0)
+        def _():
+            @pl.loop(0, HALF, unroll=8)
+            def _(t):
+                frame[16 + t, EDGE_LOW, :] = recv_l[index, t].astype(F32)
 
         @pl.loop(0, HALF, unroll=8)
         def _(t):
-            frame[16 + t, EDGE_LOW, :] = recv_l[index, t].astype(F32)
             frame[16 + t, EDGE_HIGH, :] = recv_r[index, t].astype(F32)
+
+    def put_down_left(index, k, value):
+        recv_c[index, FAR_BELOW - 4, k] = value.astype(BF16)
+
+    def unpack_forward(index):
+        @pl.when(off == 0)
+        def _():
+            def put_left(t, value):
+                frame[16 + t, EDGE_LOW, :] = value
+
+            rows_to_cols(lambda k: recv_a[index, k].astype(F32), put_left)
+            turn_corner(
+                lambda k: recv_c[index, FAR_ABOVE - 4, k].astype(F32),
+                functools.partial(put_down_left, index),
+            )
 
         @pl.loop(0, 8, unroll=8)
         def _(k):
@@ -371,12 +382,12 @@
                         low, 0.0, other
                     ).astype(BF16)
 
-    def shift_columns(layer):
+    def shift_columns(layer, tiles, which):
         spread = dilation_ref[layer]
 
-        @pl.loop(0, 64, unroll=4)
+        @pl.loop(*tiles, unroll=4)
         def _(t):
-            for b in range(3):
+            for b in which:
                 cols[layer, t, :, b * LANES : (b + 1) * LANES] = frame[
                     t, pl.ds(DMAX + (b - 1) * spread, BLOCK), :
                 ].astype(BF16)
@@ -440,9 +451,14 @@
         grad[2 * k + 1] = tiles[BLOCK:]
 
     for layer in range(LAYERS):
-        wait(layer, range(8))
+        wait(layer, (RIGHT, LEFT))
+        unpack_sides(layer)
+        shift_columns(layer, (16, 48), (1, 2))
+        wait(layer, (ABOVE, BELOW, CORNER_ABOVE, FAR_ABOVE, FAR_BELOW, CORNER_BELOW))
         unpack_forward(layer)
-        shift_columns(layer)
+        shift_columns(layer, (16, 48), (0,))
+        shift_columns(layer, (0, 16), range(3))
+        shift_columns(layer, (48, 64), range(3))
         forward(layer)
         if layer < LAYERS - 1:
             pack_forward(layer + 1)
@@ -593,7 +609,7 @@
         add(32 + k, frame[k, part, :], True)
         add(40 + k, frame[8 + k, part, :], True)
 
-    def unpack_backward(index):
+    def unpack_back_sides(index):
         @pl.loop(0, HALF, unroll=8)
         def _(t):
             total = grad[t] + frame[16 + t, CENTRE, :]
@@ -602,6 +618,7 @@
             edge = jnp.concatenate([right, jnp.zeros((32, LANES), F32), left], axis=0)
             grad[t] = total + edge
 
+    def unpack_backward(index):
         @pl.loop(0, 8, unroll=8)
         def _(k):
             def strip(ref, low, high):
@@ -678,13 +695,13 @@
             for step in peers(0):
                 sum_copy(0, step).wait_recv()
                 total = total + slots[step].astype(F32)
-            shards[mine] = total
+            shards[mine] = total.astype(BF16)
         elif stage == 2:
             for step in peers(1):
                 sum_copy(1, step).wait_recv()
-            total = shards[0]
+            total = shards[0].astype(F32)
             for at in range(1, many):
-                total = total + shards[at]
+                total = total + shards[at].astype(F32)
             whole[inner] = (total * scale).astype(BF16)
         for step in peers(stage):
             sum_copy(stage, step).start()
@@ -723,7 +740,9 @@
             def _(k):
                 from_tiles(out_ref, k, last[2 * k], last[2 * k + 1])
 
-        wait(index, range(8))
+        wait(index, (RIGHT, LEFT))
+        unpack_back_sides(index)
+        wait(index, (ABOVE, BELOW, CORNER_ABOVE, FAR_ABOVE, FAR_BELOW, CORNER_BELOW))
         unpack_backward(index)
 
     @pl.loop(0, 16, unroll=4)
@@ -785,7 +804,7 @@
             pltpu.VMEM((HALF, BLOCK, LANES), F32),
             pltpu.VMEM((group, *shard), BF16),
             pltpu.VMEM((group, *shard), BF16),
-            pltpu.VMEM((many, *shard), F32),
+            pltpu.VMEM((many, *shard), BF16),
             pltpu.VMEM((group, *shard), BF16),
             pltpu.VMEM((LAYERS, 64, BLOCK, 3 * LANES), BF16),
             pltpu.VMEM((LAYERS, HALF, BLOCK, 2 * LANES), F32),
@@ -819,7 +838,7 @@
         name="net",
     )(
         band_width,
-        dilation,
+        pltpu.with_memory_space_constraint(dilation, pltpu.HBM),
         pltpu.with_memory_space_constraint(input_map.reshape(CH, bins), pltpu.HBM),
         pltpu.with_memory_space_constraint(cotangent.reshape(CH, bins), pltpu.HBM),
         pltpu.with_memory_space_constraint(conv_weight, pltpu.HBM),

time: 65.4 us -> 63.6 us (0.972)
  Pallas kernels: 63.1 us -> 61.9 us
    pallas_call x1, Pallas kernels: 61.7 us -> 60.5 us  [per_device(): pl.pallas_call(functools.partial(net_kernel, rows_all, offsets_all, scale...]
where the time goes in v3:
time: 63.6 us; the launch traced here: 63.3 us
  Pallas kernels  61.9 us (97%)
  between operations  1.45 us (2%)
    pallas_call x1, Pallas kernels, per_device(): pl.pallas_call(functools.partial(net_kernel, rows_all, offsets_all, scale...  60.5 us
    pallas_call x1, Pallas kernels, per_device(): pl.pallas_call(finish_kernel, out_shape=shapes, in_specs=[vmem] * 4, out_...  1.39 us

profile of v3, /device:TPU:1, one launch (start us, length us, event | category | flops | bytes accessed | tf_op | source)
XLA Modules:
  0.0 63.3 jit_solution(16967540662721020054)
XLA Ops:
  1.3 60.5 %net.1 = (bf16[64,4096]{1,0:T(8,128)(2,1)S(1)}, f32[64,4096]{1,0:T(8,128)S(1)}, f32[2,64,576]{2,1,0:T(8,128)S(1)}, f32[2,64]{1,0:T(2,128)S(1)}) custom-call(s32[1]{0:T(128)S(6)} %copy.10.width_ref, s32[2]{0:T(128)} %dilation_ref.1, bf16[64,4096]{1,0:T(8,128)(2,1)} %bitcast.4, bf16[64,4096]{1,0:T(8,128)(2,1)} %bitcast.5, bf16[2,64,576]{2,1,0:T(8,128)(2,1)} %weight_hbm.1, ...), custom_call_target="tpu_custom_call" | custom-call | tf_op jit(solution)/shard_map/net/pallas_call | solution.py:792
  61.8 1.4 %finish.1 = (bf16[64,4096]{1,0:T(8,128)(2,1)}, f32[64,4096]{1,0:T(8,128)}, f32[2,64,576]{2,1,0:T(8,128)}, f32[2,64]{1,0:T(2,128)}) custom-call(bf16[64,4096]{1,0:T(8,128)(2,1)S(1)} %get-tuple-element.12.refs_0_, f32[64,4096]{1,0:T(8,128)S(1)} %get-tuple-element.13.refs_1_, f32[2,64,576]{2,1,0:T(8,128)S(1)} %get-tuple-element.14.refs_2_, ...), custom_call_target="tpu_custom_call" | custom-call | tf_op jit(solution)/shard_map/finish/pallas_call | solution.py:848

commit v4 on v3

--- a/solution.py
+++ b/solution.py
@@ -689,22 +689,36 @@
     def peers(stage):
         return range(1, many if stage == 1 else group)
 
-    def sum_start(stage):
-        if stage == 1:
-            total = term_ref[inner].astype(F32)
+    def of_layer(slab, layer):
+        return lax.div(slab, group // LAYERS) == layer
+
+    def sum_start(stage, layer):
+        if stage == 0:
             for step in peers(0):
-                sum_copy(0, step).wait_recv()
-                total = total + slots[step].astype(F32)
-            shards[mine] = total.astype(BF16)
-        elif stage == 2:
-            for step in peers(1):
-                sum_copy(1, step).wait_recv()
-            total = shards[0].astype(F32)
-            for at in range(1, many):
-                total = total + shards[at].astype(F32)
-            whole[inner] = (total * scale).astype(BF16)
-        for step in peers(stage):
-            sum_copy(stage, step).start()
+
+                @pl.when(of_layer(in_plane(step)[0], layer))
+                def _():
+                    sum_copy(0, step).start()
+
+            return
+
+        @pl.when(of_layer(inner, layer))
+        def _():
+            if stage == 1:
+                total = term_ref[inner].astype(F32)
+                for step in peers(0):
+                    sum_copy(0, step).wait_recv()
+                    total = total + slots[step].astype(F32)
+                shards[mine] = total.astype(BF16)
+            else:
+                for step in peers(1):
+                    sum_copy(1, step).wait_recv()
+                total = shards[0].astype(F32)
+                for at in range(1, many):
+                    total = total + shards[at].astype(F32)
+                whole[inner] = (total * scale).astype(BF16)
+            for step in peers(stage):
+                sum_copy(stage, step).start()
 
     def sum_end():
         for step in peers(2):
@@ -724,17 +738,21 @@
         bias_rows = slope_step(layer)
         if layer == 0:
             weight_terms(layer, bias_rows)
-            sum_start(0)
+            sum_start(0, 0)
         edge = 64 // BWD // 4
         tile_grad(layer, (*range(edge), *range(3 * edge, 4 * edge)))
         pack_outer(index)
+        if layer == 0:
+            sum_start(1, 1)
         tile_grad(layer, range(edge, 3 * edge))
         pack_centre(index)
         if layer == 0:
-            sum_start(1)
-            sum_start(2)
+            sum_start(2, 1)
+            sum_start(1, 0)
+            sum_start(2, 0)
         else:
             weight_terms(layer, bias_rows)
+            sum_start(0, 1)
 
             @pl.loop(0, 16, unroll=4)
             def _(k):

time: 63.6 us -> 62 us (0.975)
  Pallas kernels: 61.9 us -> 60.4 us
    pallas_call x1, Pallas kernels: 60.5 us -> 59 us  [per_device(): pl.pallas_call(functools.partial(net_kernel, rows_all, offsets_all, scale...]
where the time goes in v4:
time: 62 us; the launch traced here: 61.8 us
  Pallas kernels  60.4 us (97%)
  between operations  1.45 us (2%)
    pallas_call x1, Pallas kernels, per_device(): pl.pallas_call(functools.partial(net_kernel, rows_all, offsets_all, scale...  59 us
    pallas_call x1, Pallas kernels, per_device(): pl.pallas_call(finish_kernel, out_shape=shapes, in_specs=[vmem] * 4, out_...  1.39 us

profile of v4, /device:TPU:1, one launch (start us, length us, event | category | flops | bytes accessed | tf_op | source)
XLA Modules:
  0.0 61.8 jit_solution(6552196777847817569)
XLA Ops:
  1.3 59.0 %net.1 = (bf16[64,4096]{1,0:T(8,128)(2,1)S(1)}, f32[64,4096]{1,0:T(8,128)S(1)}, f32[2,64,576]{2,1,0:T(8,128)S(1)}, f32[2,64]{1,0:T(2,128)S(1)}) custom-call(s32[1]{0:T(128)S(6)} %copy.10.width_ref, s32[2]{0:T(128)} %dilation_ref.1, bf16[64,4096]{1,0:T(8,128)(2,1)} %bitcast.4, bf16[64,4096]{1,0:T(8,128)(2,1)} %bitcast.5, bf16[2,64,576]{2,1,0:T(8,128)(2,1)} %weight_hbm.1, ...), custom_call_target="tpu_custom_call" | custom-call | tf_op jit(solution)/shard_map/net/pallas_call | solution.py:810
  60.3 1.4 %finish.1 = (bf16[64,4096]{1,0:T(8,128)(2,1)}, f32[64,4096]{1,0:T(8,128)}, f32[2,64,576]{2,1,0:T(8,128)}, f32[2,64]{1,0:T(2,128)}) custom-call(bf16[64,4096]{1,0:T(8,128)(2,1)S(1)} %get-tuple-element.12.refs_0_, f32[64,4096]{1,0:T(8,128)S(1)} %get-tuple-element.13.refs_1_, f32[2,64,576]{2,1,0:T(8,128)S(1)} %get-tuple-element.14.refs_2_, ...), custom_call_target="tpu_custom_call" | custom-call | tf_op jit(solution)/shard_map/finish/pallas_call | solution.py:866

commit v5 on v4

--- a/solution.py
+++ b/solution.py
@@ -694,7 +694,7 @@
 
     def sum_start(stage, layer):
         if stage == 0:
-            for step in peers(0):
+            for step in far_first(0):
 
                 @pl.when(of_layer(in_plane(step)[0], layer))
                 def _():
@@ -717,8 +717,14 @@
                 for at in range(1, many):
                     total = total + shards[at].astype(F32)
                 whole[inner] = (total * scale).astype(BF16)
-            for step in peers(stage):
+            for step in far_first(stage):
                 sum_copy(stage, step).start()
+
+    def far_first(stage):
+        def hops(step):
+            return min(step % 4, -step % 4) + min(step // 4, -(step // 4) % 4)
+
+        return sorted(peers(stage), key=hops, reverse=True)
 
     def sum_end():
         for step in peers(2):

time: 62 us -> 60.6 us (0.977)
  Pallas kernels: 60.4 us -> 58.8 us
    pallas_call x1, Pallas kernels: 59 us -> 57.4 us  [per_device(): pl.pallas_call(functools.partial(net_kernel, rows_all, offsets_all, scale...]
where the time goes in v5:
time: 60.6 us; the launch traced here: 60.3 us
  Pallas kernels  58.8 us (97%)
  between operations  1.45 us (2%)
    pallas_call x1, Pallas kernels, per_device(): pl.pallas_call(functools.partial(net_kernel, rows_all, offsets_all, scale...  57.4 us
    pallas_call x1, Pallas kernels, per_device(): pl.pallas_call(finish_kernel, out_shape=shapes, in_specs=[vmem] * 4, out_...  1.39 us

profile of v5, /device:TPU:1, one launch (start us, length us, event | category | flops | bytes accessed | tf_op | source)
XLA Modules:
  0.0 60.3 jit_solution(7816301554076870913)
XLA Ops:
  1.3 57.4 %net.1 = (bf16[64,4096]{1,0:T(8,128)(2,1)S(1)}, f32[64,4096]{1,0:T(8,128)S(1)}, f32[2,64,576]{2,1,0:T(8,128)S(1)}, f32[2,64]{1,0:T(2,128)S(1)}) custom-call(s32[1]{0:T(128)S(6)} %copy.10.width_ref, s32[2]{0:T(128)} %dilation_ref.1, bf16[64,4096]{1,0:T(8,128)(2,1)} %bitcast.4, bf16[64,4096]{1,0:T(8,128)(2,1)} %bitcast.5, bf16[2,64,576]{2,1,0:T(8,128)(2,1)} %weight_hbm.1, ...), custom_call_target="tpu_custom_call" | custom-call | tf_op jit(solution)/shard_map/net/pallas_call | solution.py:816
  58.7 1.4 %finish.1 = (bf16[64,4096]{1,0:T(8,128)(2,1)}, f32[64,4096]{1,0:T(8,128)}, f32[2,64,576]{2,1,0:T(8,128)}, f32[2,64]{1,0:T(2,128)}) custom-call(bf16[64,4096]{1,0:T(8,128)(2,1)S(1)} %get-tuple-element.12.refs_0_, f32[64,4096]{1,0:T(8,128)S(1)} %get-tuple-element.13.refs_1_, f32[2,64,576]{2,1,0:T(8,128)S(1)} %get-tuple-element.14.refs_2_, ...), custom_call_target="tpu_custom_call" | custom-call | tf_op jit(solution)/shard_map/finish/pallas_call | solution.py:872

commit v6 on v5

--- a/solution.py
+++ b/solution.py
@@ -26,6 +26,9 @@
 EDGE_LOW = slice(0, DMAX)
 CENTRE = slice(DMAX, DMAX + BLOCK)
 EDGE_HIGH = slice(DMAX + BLOCK, WIDE)
+FARTHEST_FIRST = (
+    RIGHT, LEFT, FAR_ABOVE, FAR_BELOW, ABOVE, BELOW, CORNER_ABOVE, CORNER_BELOW
+)
 SQRT_2_PI = math.sqrt(2.0 / math.pi)
 CUBIC = 0.044715
 
@@ -437,7 +440,7 @@
 
     pack_forward(0)
     pl.semaphore_wait(barrier, count)
-    send(0, range(8))
+    send(0, FARTHEST_FIRST)
     loads[1].wait()
     loads[2].wait()
     for layer in range(LAYERS):
@@ -462,7 +465,7 @@
         forward(layer)
         if layer < LAYERS - 1:
             pack_forward(layer + 1)
-            send(layer + 1, range(8))
+            send(layer + 1, FARTHEST_FIRST)
 
     @pl.loop(0, 16, unroll=4)
     def _(t):
@@ -543,7 +546,7 @@
         def _():
             send_above(index)
 
-        send(index, (BELOW, CORNER_ABOVE, FAR_ABOVE, FAR_BELOW, CORNER_BELOW))
+        send(index, (FAR_ABOVE, FAR_BELOW, BELOW, CORNER_ABOVE, CORNER_BELOW))
 
     def send_above(index):
         @pl.loop(0, 8, unroll=8)
@@ -722,6 +725,8 @@
 
     def far_first(stage):
         def hops(step):
+            if stage == 1:
+                return min(step, many - step)
             return min(step % 4, -step % 4) + min(step // 4, -(step // 4) % 4)
 
         return sorted(peers(stage), key=hops, reverse=True)

time: 60.6 us -> 60.9 us (level)
  no operation moved by 1% of the time
where the time goes in v6:
time: 60.9 us; the launch traced here: 60.6 us
  Pallas kernels  59.1 us (97%)
  between operations  1.45 us (2%)
    pallas_call x1, Pallas kernels, per_device(): pl.pallas_call(functools.partial(net_kernel, rows_all, offsets_all, scale...  57.7 us
    pallas_call x1, Pallas kernels, per_device(): pl.pallas_call(finish_kernel, out_shape=shapes, in_specs=[vmem] * 4, out_...  1.39 us

profile of v6, /device:TPU:1, one launch (start us, length us, event | category | flops | bytes accessed | tf_op | source)
XLA Modules:
  0.0 60.6 jit_solution(14989272740446136917)
XLA Ops:
  1.3 57.7 %net.1 = (bf16[64,4096]{1,0:T(8,128)(2,1)S(1)}, f32[64,4096]{1,0:T(8,128)S(1)}, f32[2,64,576]{2,1,0:T(8,128)S(1)}, f32[2,64]{1,0:T(2,128)S(1)}) custom-call(s32[1]{0:T(128)S(6)} %copy.10.width_ref, s32[2]{0:T(128)} %dilation_ref.1, bf16[64,4096]{1,0:T(8,128)(2,1)} %bitcast.4, bf16[64,4096]{1,0:T(8,128)(2,1)} %bitcast.5, bf16[2,64,576]{2,1,0:T(8,128)(2,1)} %weight_hbm.1, ...), custom_call_target="tpu_custom_call" | custom-call | tf_op jit(solution)/shard_map/net/pallas_call | solution.py:821
  59.0 1.4 %finish.1 = (bf16[64,4096]{1,0:T(8,128)(2,1)}, f32[64,4096]{1,0:T(8,128)}, f32[2,64,576]{2,1,0:T(8,128)}, f32[2,64]{1,0:T(2,128)}) custom-call(bf16[64,4096]{1,0:T(8,128)(2,1)S(1)} %get-tuple-element.12.refs_0_, f32[64,4096]{1,0:T(8,128)S(1)} %get-tuple-element.13.refs_1_, f32[2,64,576]{2,1,0:T(8,128)S(1)} %get-tuple-element.14.refs_2_, ...), custom_call_target="tpu_custom_call" | custom-call | tf_op jit(solution)/shard_map/finish/pallas_call | solution.py:877
